TPU v7x, 512 devices: a whole 4x4x16 slice. The times are simulated.
512 devices in a mesh: dp: 64 (over z, y), feat: 8 (over x, core).
Axes of the slice: x: 4, y: 4, z: 16, core: 2. Of those that a mesh axis runs over, the one named last changes fastest.
Arguments:
- points: float32 [65536, 256], P('dp'), may hold values from -6 to 6
- frequencies: float32 [256, 1024], P(None, 'feat'), may hold values from -0.5 to 0.5
- halton_start: int32 [1], replicated, may hold values from 0 to 39999
Outputs:
- scores: float32 [65536], P(('dp', 'feat'))
- r_factor: float32 [1024, 1024], P(None, 'feat')
All inputs are finite; a program needn't handle non-finite values.
Results may differ from a plain program's by a relative error of at most 0.0003.
Values sent between devices are 32-bit elements; how exact they have to be, the bound alone decides.
A program may use at most 64 MiB of HBM per device.

v0:
```python
import math
import jax
import jax.numpy as jnp
from jax import lax
from jax.sharding import PartitionSpec as P

ridge_level = 0.1


def halton_phase(halton_start, columns):
    index_value = halton_start[0] + columns
    radical = jnp.zeros(columns.shape, jnp.float32)
    for place in range(16):
        digit_bit = index_value // (1 << place) % 2
        radical = radical + digit_bit.astype(jnp.float32) * 0.5 ** (place + 1)
    return 2.0 * math.pi * radical


def featurize(row_block, frequencies, phase):
    angles = jnp.dot(
        row_block, frequencies, precision=lax.Precision.HIGHEST, preferred_element_type=jnp.float32
    )
    return math.sqrt(2.0) * jnp.cos(angles + phase)


def per_device(points, frequencies, halton_start):
    panel_width = frequencies.shape[1]
    feat_count = lax.axis_size("feat")
    group_count = lax.axis_size("dp")
    feat_total = panel_width * feat_count
    row_count = points.shape[0]
    total_rows = row_count * group_count
    feat_place = lax.axis_index("feat")
    columns = feat_place * panel_width + jnp.arange(panel_width, dtype=jnp.int32)
    own_panel = featurize(points, frequencies, halton_phase(halton_start, columns))
    gram_block = jnp.dot(
        lax.all_gather(own_panel, "feat", axis=1, tiled=True).T,
        own_panel,
        precision=lax.Precision.HIGHEST,
        preferred_element_type=jnp.float32,
    )
    own_rows = lax.all_to_all(own_panel, "feat", split_axis=0, concat_axis=1, tiled=True)
    summed = lax.psum(gram_block, "dp")
    gram_total = lax.all_gather(summed, "feat", axis=1, tiled=True)
    gram_full = gram_total / total_rows + ridge_level * jnp.eye(feat_total, dtype=jnp.float32)
    factor = jnp.linalg.cholesky(gram_full)
    solved = lax.linalg.triangular_solve(factor, own_rows.T, left_side=True, lower=True)
    scores = jnp.sum(solved * solved, axis=0) / feat_total
    own_factor = lax.dynamic_slice_in_dim(factor, feat_place * panel_width, panel_width, 1)
    return (scores, own_factor)


def solution(mesh):
    in_specs = (P("dp", None), P(None, "feat"), P())
    out_specs = (P(("dp", "feat")), P(None, "feat"))
    return jax.shard_map(
        per_device, mesh=mesh, in_specs=in_specs, out_specs=out_specs, check_vma=False
    )
```

profile of v0, /device:TPU:1, one launch (start us, length us, event | category | flops | bytes accessed | tf_op | source)
XLA Modules:
  0.0 727.1 jit_solution(13208123939911550002)
XLA Ops:
  12.8 49.5 %all-gather.3.cloned.1.call-done = f32[1024,1024]{1,0:T(8,128)} async-done(((f32[1024,128]{1,0:T(8,128)}), f32[1024,1024]{1,0:T(8,128)}) %all-gather.3.cloned.1.call-update) | async-done | bytes 4194320 | tf_op jit(solution)/shard_map/all_gather | solution.py:37
  62.3 5.6 fusion.128
  68.0 256.7 %all-reduce.3.cloned.1.call-done = f32[1024,128]{0,1:T(8,128)} async-done(((f32[1024,128]{0,1:T(8,128)}), f32[1024,128]{0,1:T(8,128)}) %all-reduce.3.cloned.1.call-update) | async-done | bytes 524304 | tf_op jit(solution)/shard_map/psum | solution.py:43
  325.7 15.0 %all-to-all-start = ((f32[8,128,128]{1,2,0:T(8,128)}), f32[8,128,128]{1,2,0:T(8,128)S(1)}, u32[]{:S(2)}, u32[]{:S(2)}) async-start(f32[8,128,128]{1,2,0:T(8,128)} %copy.42), calls=%async_computation | async-start | bytes 1048576 | tf_op jit(solution)/shard_map/all_to_all | solution.py:42
  340.7 31.0 %all-gather.5.cloned.1.call-done = f32[1024,1024]{0,1:T(8,128)} async-done(((f32[1024,128]{0,1:T(8,128)}), f32[1024,1024]{0,1:T(8,128)}) %all-gather.5.cloned.1.call-update) | async-done | bytes 4194320 | tf_op jit(solution)/shard_map/all_gather | solution.py:44
  376.7 5.8 copy.25
  388.9 11.7 %cholesky.222 = f32[128,128]{1,0:T(8,128)S(1)} custom-call(f32[128,128]{1,0:T(8,128)S(1)} %cholesky.577), custom_call_target="Cholesky" | custom-call | tf_op jit(solution)/shard_map/jit(cholesky)/cholesky | solution.py:46
  400.8 9.8 %custom-call.62 = f32[1,128,128]{1,2,0:T(8,128)S(1)} custom-call(f32[1,128,128]{2,1,0:T(8,128)S(1)} %get-tuple-element.72), custom_call_target="InvertDiagBlocksLowerTriangular" | custom-call | tf_op jit(solution)/shard_map/jit(cholesky)/cholesky | solution.py:46
  413.9 11.7 %cholesky.243 = f32[128,128]{1,0:T(8,128)S(1)} custom-call(f32[128,128]{1,0:T(8,128)S(1)} %cholesky.581), custom_call_target="Cholesky" | custom-call | tf_op jit(solution)/shard_map/jit(cholesky)/cholesky | solution.py:46
  425.9 9.8 %custom-call.63 = f32[1,128,128]{1,2,0:T(8,128)S(1)} custom-call(f32[1,128,128]{2,1,0:T(8,128)S(1)} %get-tuple-element.70), custom_call_target="InvertDiagBlocksLowerTriangular" | custom-call | tf_op jit(solution)/shard_map/jit(cholesky)/cholesky | solution.py:46
  441.3 11.7 %cholesky.466 = f32[128,128]{1,0:T(8,128)S(1)} custom-call(f32[128,128]{1,0:T(8,128)S(1)} %cholesky.586), custom_call_target="Cholesky" | custom-call | tf_op jit(solution)/shard_map/jit(cholesky)/cholesky | solution.py:46
  453.7 9.8 %custom-call.64 = f32[1,128,128]{1,2,0:T(8,128)S(1)} custom-call(f32[1,128,128]{2,1,0:T(8,128)S(1)} %get-tuple-element.68), custom_call_target="InvertDiagBlocksLowerTriangular" | custom-call | tf_op jit(solution)/shard_map/jit(cholesky)/cholesky | solution.py:46
  468.1 11.7 %cholesky.485 = f32[128,128]{1,0:T(8,128)S(1)} custom-call(f32[128,128]{1,0:T(8,128)S(1)} %cholesky.591), custom_call_target="Cholesky" | custom-call | tf_op jit(solution)/shard_map/jit(cholesky)/cholesky | solution.py:46
  480.6 9.8 %custom-call.65 = f32[1,128,128]{1,2,0:T(8,128)S(1)} custom-call(f32[1,128,128]{2,1,0:T(8,128)S(1)} %get-tuple-element.66), custom_call_target="InvertDiagBlocksLowerTriangular" | custom-call | tf_op jit(solution)/shard_map/jit(cholesky)/cholesky | solution.py:46
  494.7 12.1 %cholesky.504 = f32[128,128]{1,0:T(8,128)S(1)} custom-call(f32[128,128]{1,0:T(8,128)S(1)} %cholesky.596), custom_call_target="Cholesky" | custom-call | tf_op jit(solution)/shard_map/jit(cholesky)/cholesky | solution.py:46
  507.6 9.8 %custom-call.66 = f32[1,128,128]{1,2,0:T(8,128)S(1)} custom-call(f32[1,128,128]{2,1,0:T(8,128)S(1)} %get-tuple-element.64), custom_call_target="InvertDiagBlocksLowerTriangular" | custom-call | tf_op jit(solution)/shard_map/jit(cholesky)/cholesky | solution.py:46
  521.8 11.7 %cholesky.524 = f32[128,128]{1,0:T(8,128)S(1)} custom-call(f32[128,128]{1,0:T(8,128)S(1)} %cholesky.601), custom_call_target="Cholesky" | custom-call | tf_op jit(solution)/shard_map/jit(cholesky)/cholesky | solution.py:46
  534.3 9.8 %custom-call.67 = f32[1,128,128]{1,2,0:T(8,128)S(1)} custom-call(f32[1,128,128]{2,1,0:T(8,128)S(1)} %get-tuple-element.62), custom_call_target="InvertDiagBlocksLowerTriangular" | custom-call | tf_op jit(solution)/shard_map/jit(cholesky)/cholesky | solution.py:46
  548.0 11.7 %cholesky.544 = f32[128,128]{1,0:T(8,128)S(1)} custom-call(f32[128,128]{1,0:T(8,128)S(1)} %cholesky.606), custom_call_target="Cholesky" | custom-call | tf_op jit(solution)/shard_map/jit(cholesky)/cholesky | solution.py:46
  560.5 9.8 %custom-call.68 = f32[1,128,128]{1,2,0:T(8,128)S(1)} custom-call(f32[1,128,128]{2,1,0:T(8,128)S(1)} %get-tuple-element.60), custom_call_target="InvertDiagBlocksLowerTriangular" | custom-call | tf_op jit(solution)/shard_map/jit(cholesky)/cholesky | solution.py:46
  573.4 11.7 %cholesky.562 = f32[128,128]{1,0:T(8,128)S(1)} custom-call(f32[128,128]{1,0:T(8,128)S(1)} %convolution_subtract_fusion.11), custom_call_target="Cholesky" | custom-call | tf_op jit(solution)/shard_map/jit(cholesky)/cholesky | solution.py:46
  595.7 6.6 fusion.1
  602.2 23.6 %while.1 = (s32[]{:T(128)}, f32[1024,1024]{0,1:T(8,128)}, s32[8,2]{0,1:T(2,128)S(1)}, f32[8,128,128]{2,1,0:T(8,128)S(1)}, s32[]{:T(128)}) while((s32[]{:T(128)}, f32[1024,1024]{0,1:T(8,128)}, s32[8,2]{0,1:T(2,128)S(1)}, f32[8,128,128]{2,1,0:T(8,128)S(1)}, s32[]{:T(128)}) %tuple.58), condition=%wide.while_cond, body=%wide.while_body.sunk | while | flops 2 | bytes 393329 | solution.py:47
  625.8 78.6 %custom-call.69 = f32[8,128,128]{1,2,0:T(8,128)S(1)} custom-call(f32[8,128,128]{2,1,0:T(8,128)S(1)} %get-tuple-element.9), custom_call_target="InvertDiagBlocksLowerTriangular" | custom-call | tf_op jit(solution)/shard_map/triangular_solve | solution.py:47
  (136 shorter events, 95.0 us)
Async XLA Ops:
  7.2 1.2 copy-start
  7.2 55.1 %all-gather.3.cloned.1.call-start = ((), (), s32[]{:S(2)}) async-start(), calls=%async_computation.1 | async-start | bytes 4718592 | tf_op jit(solution)/shard_map/all_gather | solution.py:37
  12.7 312.0 %copy-start.3 = (f32[1024,128]{1,0:T(8,128)S(1)}, f32[1024,128]{1,0:T(8,128)}, u32[]{:S(2)}) copy-start(f32[1024,128]{1,0:T(8,128)} %fusion.3) | copy-start | bytes 1572868
  12.7 312.0 %all-reduce.3.cloned.1.call-start = ((), (), s32[]{:S(2)}) async-start(), calls=%async_computation.2 | async-start | bytes 1048576 | tf_op jit(solution)/shard_map/psum | solution.py:43
  68.0 303.7 %all-gather.5.cloned.1.call-start = ((), (), s32[]{:S(2)}) async-start(), calls=%async_computation.3 | async-start | bytes 4718592 | tf_op jit(solution)/shard_map/all_gather | solution.py:44
  325.7 378.7 %all-to-all-start = ((f32[8,128,128]{1,2,0:T(8,128)}), f32[8,128,128]{1,2,0:T(8,128)S(1)}, u32[]{:S(2)}, u32[]{:S(2)}) async-start(f32[8,128,128]{1,2,0:T(8,128)} %copy.42), calls=%async_computation | async-start | bytes 1048576 | tf_op jit(solution)/shard_map/all_to_all | solution.py:42
  387.0 1.9 copy-start.2
  436.8 2.0 copy-start.1
Sparse Core Ops, SparseCore 0:
  12.8 49.4 all-gather.2
  68.1 256.5 all-reduce.2
  327.1 44.5 all-gather.4
where the time goes:
time: 733 us; the launch traced here: 727 us
  waiting for transfers between devices  337 us (46%)
  other arithmetic  263 us (36%)
  matrix products  49.2 us (7%)
  local copies, waits for them, and re-layouts  41.8 us (6%)
  between operations  20.1 us (3%)
  starting transfers between devices  15.1 us (2%)
    psum x1, waiting for transfers between devices, per_device(): summed = lax.psum(gram_block, 'dp')  257 us
    another operation x30, other arithmetic, per_device(): factor = jnp.linalg.cholesky(gram_full)  168 us
    another operation x3, other arithmetic, per_device(): lax.linalg.triangular_solve(factor, own_rows.T, left_side=True, lower=True)  85.2 us
    all_gather x1, waiting for transfers between devices, per_device(): lax.all_gather(own_panel, 'feat', axis=1, tiled=True)  49.5 us
    all_gather x1, waiting for transfers between devices, per_device(): gram_total = lax.all_gather(summed, 'feat', axis=1, tiled=True)  31 us
    another operation x14, matrix products, per_device(): factor = jnp.linalg.cholesky(gram_full)  26.2 us
    another operation x40, local copies, waits for them, and re-layouts  23.1 us
    all_to_all x1, starting transfers between devices, per_device(): lax.all_to_all(own_panel, 'feat', split_axis=0, concat_axis=1, tiled=True)  15 us
  transfers between devices with their start and end apart: 4, of which 3 were waited for; matrix products, arithmetic and copies ran while one was open for 45% of the time, Pallas kernels for 0%

commit v1 on v0

--- a/solution.py
+++ b/solution.py
@@ -3,6 +3,7 @@
 import jax.numpy as jnp
 from jax import lax
 from jax.sharding import PartitionSpec as P
+from jax.lax import all_gather
 
 ridge_level = 0.1
 
@@ -40,7 +41,7 @@
         preferred_element_type=jnp.float32,
     )
     own_rows = lax.all_to_all(own_panel, "feat", split_axis=0, concat_axis=1, tiled=True)
-    summed = lax.psum(gram_block, "dp")
+    summed = jnp.sum(all_gather(gram_block, "dp"), axis=0)
     gram_total = lax.all_gather(summed, "feat", axis=1, tiled=True)
     gram_full = gram_total / total_rows + ridge_level * jnp.eye(feat_total, dtype=jnp.float32)
     factor = jnp.linalg.cholesky(gram_full)

time: 733 us -> 783 us (1.068)
  waiting for transfers between devices: 337 us -> 375 us
  other arithmetic: 263 us -> 275 us
  starting transfers between devices: 15.1 us -> 5.45 us
    all_gather x0 -> x1, waiting for transfers between devices: none -> 295 us  [per_device(): summed = jnp.sum(all_gather(gram_block, 'dp'), axis=0)]
    psum x1 -> x0, waiting for transfers between devices: 257 us -> none  [per_device(): summed = lax.psum(gram_block, 'dp')]
    reduce_sum x0 -> x1, other arithmetic: none -> 11.7 us  [per_device(): summed = jnp.sum(all_gather(gram_block, 'dp'), axis=0)]
    all_to_all x1, starting transfers between devices: 15 us -> 5.33 us  [per_device(): lax.all_to_all(own_panel, 'feat', split_axis=0, concat_axis=1, tiled=True)]
  transfers between devices with their start and end apart: 4 -> 4, of which waited for: 3 -> 3; matrix products, arithmetic and copies ran while one was open for 45% -> 42% of each run, Pallas kernels for 0% -> 0%
where the time goes in v1:
time: 783 us; the launch traced here: 775 us
  waiting for transfers between devices  375 us (48%)
  other arithmetic  275 us (35%)
  matrix products  54.4 us (7%)
  local copies, waits for them, and re-layouts  44.3 us (6%)
  between operations  20.1 us (3%)
    all_gather x1, waiting for transfers between devices, per_device(): summed = jnp.sum(all_gather(gram_block, 'dp'), axis=0)  295 us
    another operation x30, other arithmetic, per_device(): factor = jnp.linalg.cholesky(gram_full)  168 us
    another operation x3, other arithmetic, per_device(): lax.linalg.triangular_solve(factor, own_rows.T, left_side=True, lower=True)  85.2 us
    all_gather x1, waiting for transfers between devices, per_device(): lax.all_gather(own_panel, 'feat', axis=1, tiled=True)  49.5 us
    all_gather x1, waiting for transfers between devices, per_device(): gram_total = lax.all_gather(summed, 'feat', axis=1, tiled=True)  30.8 us
    another operation x14, matrix products, per_device(): factor = jnp.linalg.cholesky(gram_full)  27.3 us
    another operation x40, local copies, waits for them, and re-layouts  23.1 us
  transfers between devices with their start and end apart: 4, of which 3 were waited for; matrix products, arithmetic and copies ran while one was open for 42% of the time, Pallas kernels for 0%

profile of v1, /device:TPU:1, one launch (start us, length us, event | category | flops | bytes accessed | tf_op | source)
XLA Modules:
  0.0 774.8 jit_solution(11647475211474520326)
XLA Ops:
  12.8 49.5 %all-gather.5.cloned.1.call-done = f32[1024,1024]{1,0:T(8,128)} async-done(((f32[1024,128]{1,0:T(8,128)}), f32[1024,1024]{1,0:T(8,128)}) %all-gather.5.cloned.1.call-update) | async-done | bytes 4194320 | tf_op jit(solution)/shard_map/all_gather | solution.py:38
  62.3 9.8 %fusion.128 = f32[1024,128]{1,0:T(8,128)} fusion(f32[1024,1024]{1,0:T(8,128)} %all-gather.5.cloned.1.call-done, f32[1024,128]{1,0:T(8,128)} %fusion.3), kind=kOutput, calls=%fused_computation.320 | convolution fusion | flops 1610612736 | bytes 5242880 | tf_op jit(solution)/shard_map/dot_general | solution.py:37
  72.1 294.8 %all-gather.9.cloned.1.call-done = f32[65536,128]{1,0:T(8,128)} async-done(((f32[1024,128]{1,0:T(8,128)}), f32[65536,128]{1,0:T(8,128)}) %all-gather.9.cloned.1.call-update) | async-done | bytes 33554448 | tf_op jit(solution)/shard_map/all_gather | solution.py:44
  366.9 11.7 %reduce_sum.18 = f32[1024,128]{1,0:T(8,128)S(1)} reduce(f32[64,1024,128]{2,1,0:T(8,128)} %bitcast.112, f32[]{:T(128)} %constant.572.clone.1), dimensions={0}, to_apply=%region_0.1 | reduce | flops 8257536 | bytes 34078724 | tf_op jit(solution)/shard_map/reduce_sum | solution.py:44
  386.0 30.8 %all-gather.7.cloned.1.call-done = f32[1024,1024]{0,1:T(8,128)} async-done(((f32[1024,128]{0,1:T(8,128)}), f32[1024,1024]{0,1:T(8,128)}) %all-gather.7.cloned.1.call-update) | async-done | bytes 4194320 | tf_op jit(solution)/shard_map/all_gather | solution.py:45
  421.8 5.8 copy.43
  434.0 11.7 %cholesky.222 = f32[128,128]{1,0:T(8,128)S(1)} custom-call(f32[128,128]{1,0:T(8,128)S(1)} %cholesky.577), custom_call_target="Cholesky" | custom-call | tf_op jit(solution)/shard_map/jit(cholesky)/cholesky | solution.py:47
  445.8 9.8 %custom-call.62 = f32[1,128,128]{1,2,0:T(8,128)S(1)} custom-call(f32[1,128,128]{2,1,0:T(8,128)S(1)} %get-tuple-element.78), custom_call_target="InvertDiagBlocksLowerTriangular" | custom-call | tf_op jit(solution)/shard_map/jit(cholesky)/cholesky | solution.py:47
  458.7 11.7 %cholesky.243 = f32[128,128]{1,0:T(8,128)S(1)} custom-call(f32[128,128]{1,0:T(8,128)S(1)} %cholesky.581), custom_call_target="Cholesky" | custom-call | tf_op jit(solution)/shard_map/jit(cholesky)/cholesky | solution.py:47
  473.5 9.8 %custom-call.63 = f32[1,128,128]{1,2,0:T(8,128)S(1)} custom-call(f32[1,128,128]{2,1,0:T(8,128)S(1)} %get-tuple-element.76), custom_call_target="InvertDiagBlocksLowerTriangular" | custom-call | tf_op jit(solution)/shard_map/jit(cholesky)/cholesky | solution.py:47
  488.9 11.7 %cholesky.466 = f32[128,128]{1,0:T(8,128)S(1)} custom-call(f32[128,128]{1,0:T(8,128)S(1)} %cholesky.586), custom_call_target="Cholesky" | custom-call | tf_op jit(solution)/shard_map/jit(cholesky)/cholesky | solution.py:47
  501.4 9.8 %custom-call.64 = f32[1,128,128]{1,2,0:T(8,128)S(1)} custom-call(f32[1,128,128]{2,1,0:T(8,128)S(1)} %get-tuple-element.74), custom_call_target="InvertDiagBlocksLowerTriangular" | custom-call | tf_op jit(solution)/shard_map/jit(cholesky)/cholesky | solution.py:47
  515.8 11.7 %cholesky.485 = f32[128,128]{1,0:T(8,128)S(1)} custom-call(f32[128,128]{1,0:T(8,128)S(1)} %cholesky.591), custom_call_target="Cholesky" | custom-call | tf_op jit(solution)/shard_map/jit(cholesky)/cholesky | solution.py:47
  528.3 9.8 %custom-call.65 = f32[1,128,128]{1,2,0:T(8,128)S(1)} custom-call(f32[1,128,128]{2,1,0:T(8,128)S(1)} %get-tuple-element.72), custom_call_target="InvertDiagBlocksLowerTriangular" | custom-call | tf_op jit(solution)/shard_map/jit(cholesky)/cholesky | solution.py:47
  542.4 12.1 %cholesky.504 = f32[128,128]{1,0:T(8,128)S(1)} custom-call(f32[128,128]{1,0:T(8,128)S(1)} %cholesky.596), custom_call_target="Cholesky" | custom-call | tf_op jit(solution)/shard_map/jit(cholesky)/cholesky | solution.py:47
  555.2 9.8 %custom-call.66 = f32[1,128,128]{1,2,0:T(8,128)S(1)} custom-call(f32[1,128,128]{2,1,0:T(8,128)S(1)} %get-tuple-element.70), custom_call_target="InvertDiagBlocksLowerTriangular" | custom-call | tf_op jit(solution)/shard_map/jit(cholesky)/cholesky | solution.py:47
  569.4 11.7 %cholesky.524 = f32[128,128]{1,0:T(8,128)S(1)} custom-call(f32[128,128]{1,0:T(8,128)S(1)} %cholesky.601), custom_call_target="Cholesky" | custom-call | tf_op jit(solution)/shard_map/jit(cholesky)/cholesky | solution.py:47
  581.9 9.8 %custom-call.67 = f32[1,128,128]{1,2,0:T(8,128)S(1)} custom-call(f32[1,128,128]{2,1,0:T(8,128)S(1)} %get-tuple-element.68), custom_call_target="InvertDiagBlocksLowerTriangular" | custom-call | tf_op jit(solution)/shard_map/jit(cholesky)/cholesky | solution.py:47
  595.6 11.7 %cholesky.544 = f32[128,128]{1,0:T(8,128)S(1)} custom-call(f32[128,128]{1,0:T(8,128)S(1)} %cholesky.606), custom_call_target="Cholesky" | custom-call | tf_op jit(solution)/shard_map/jit(cholesky)/cholesky | solution.py:47
  608.1 9.8 %custom-call.68 = f32[1,128,128]{1,2,0:T(8,128)S(1)} custom-call(f32[1,128,128]{2,1,0:T(8,128)S(1)} %get-tuple-element.66), custom_call_target="InvertDiagBlocksLowerTriangular" | custom-call | tf_op jit(solution)/shard_map/jit(cholesky)/cholesky | solution.py:47
  621.0 11.7 %cholesky.562 = f32[128,128]{1,0:T(8,128)S(1)} custom-call(f32[128,128]{1,0:T(8,128)S(1)} %convolution_subtract_fusion.11), custom_call_target="Cholesky" | custom-call | tf_op jit(solution)/shard_map/jit(cholesky)/cholesky | solution.py:47
  643.3 6.6 fusion.1
  649.8 23.6 %while.1 = (s32[]{:T(128)}, f32[1024,1024]{0,1:T(8,128)}, s32[8,2]{0,1:T(2,128)S(1)}, f32[8,128,128]{2,1,0:T(8,128)S(1)}, s32[]{:T(128)}) while((s32[]{:T(128)}, f32[1024,1024]{0,1:T(8,128)}, s32[8,2]{0,1:T(2,128)S(1)}, f32[8,128,128]{2,1,0:T(8,128)S(1)}, s32[]{:T(128)}) %tuple.60), condition=%wide.while_cond, body=%wide.while_body.sunk | while | flops 2 | bytes 393321 | solution.py:48
  673.4 78.6 %custom-call.69 = f32[8,128,128]{1,2,0:T(8,128)S(1)} custom-call(f32[8,128,128]{2,1,0:T(8,128)S(1)} %get-tuple-element.9), custom_call_target="InvertDiagBlocksLowerTriangular" | custom-call | tf_op jit(solution)/shard_map/triangular_solve | solution.py:48
  (138 shorter events, 103.9 us)
Async XLA Ops:
  7.2 1.2 copy-start
  7.2 55.1 %all-gather.5.cloned.1.call-start = ((), (), s32[]{:S(2)}) async-start(), calls=%async_computation.1 | async-start | bytes 4718592 | tf_op jit(solution)/shard_map/all_gather | solution.py:38
  12.7 354.2 %all-gather.9.cloned.1.call-start = ((), (), s32[]{:S(2)}) async-start(), calls=%async_computation.3 | async-start | bytes 34078720 | tf_op jit(solution)/shard_map/all_gather | solution.py:44
  72.1 344.7 %all-gather.7.cloned.1.call-start = ((), (), s32[]{:S(2)}) async-start(), calls=%async_computation.2 | async-start | bytes 4718592 | tf_op jit(solution)/shard_map/all_gather | solution.py:45
  366.9 12.8 %copy-start.3 = (f32[1024,128]{1,0:T(8,128)S(1)}, f32[1024,128]{1,0:T(8,128)}, u32[]{:S(2)}) copy-start(f32[1024,128]{1,0:T(8,128)} %fusion.3) | copy-start | bytes 1572868
  380.7 371.3 %all-to-all-start = ((f32[8,128,128]{1,2,0:T(8,128)}), f32[8,128,128]{1,2,0:T(8,128)S(1)}, u32[]{:S(2)}, u32[]{:S(2)}) async-start(f32[8,128,128]{1,2,0:T(8,128)} %copy.60), calls=%async_computation | async-start | bytes 1048576 | tf_op jit(solution)/shard_map/all_to_all | solution.py:43
  432.1 1.9 copy-start.2
  755.0 13.0 %copy-start.1 = (f32[1024,256]{1,0:T(8,128)S(1)}, f32[1024,256]{1,0:T(8,128)}, u32[]{:S(2)}) copy-start(f32[1024,256]{1,0:T(8,128)} %param.3) | copy-start | bytes 3145732
Sparse Core Ops, SparseCore 0:
  12.8 49.4 all-gather.4
  72.2 294.6 all-gather.8
  379.8 36.9 all-gather.6
